TPU v7x, 512 devices: a whole 4x8x8 slice. The times are simulated.
512 devices in a mesh: vocab: 64 (over y, x, core), width: 8 (over z).
Axes of the slice: x: 4, y: 8, z: 8, core: 2. Of those that a mesh axis runs over, the one named last changes fastest.
Arguments:
- hidden: bfloat16 [8192, 2048], P('vocab', 'width'), may hold values from -400 to 400
- norm_gain: bfloat16 [2048], P('width'), may hold values from 0.5 to 1.5
- head_weight: bfloat16 [102400, 2048], P('vocab', 'width'), may hold values from -1 to 1
- targets: int32 [8192], P(('vocab', 'width')), may hold values from 0 to 102399
- pad_mask: int32 [8192], P(('vocab', 'width')), may hold values 0 or 1
- lengths: int32 [64], replicated, may hold values from 1 to 2048, 8192 in all
Outputs:
- entropy: float32 [8192], P(('vocab', 'width'))
- token_logprob: float32 [8192], P(('vocab', 'width'))
- seq_score: float32 [64], replicated
Inputs may be any that keep to these rules, and one draw needn't show every extreme that they name: The lengths sum to 8192.
All inputs are finite; a program needn't handle non-finite values. No bound on the sum of `pad_mask` on one device may be relied on, other than what follows from the above.
Results may differ from a plain program's by a relative error of at most 0.0031.
Values may be sent and summed in bfloat16 or wider, within the bound.
A program may use at most 64 MiB of HBM per device.

v0:
```python
import math
import jax
import jax.numpy as jnp
from jax import lax
from jax.sharding import PartitionSpec as P

epsilon = 1e-06


def merged_2(value, axis, join):
    pieces = jax.tree.map(lambda part: lax.all_gather(part, axis), value)
    head = jax.tree.map(lambda part: part[0], pieces)
    tail = jax.tree.map(lambda part: part[1:], pieces)
    total, _ = lax.scan(lambda total, piece: (join(total, piece), None), head, tail)
    return total


def summarize(logits, block_ids, first_col):
    peak = jnp.max(logits, axis=1)
    shifted = logits - peak[:, None]
    weights = jnp.exp(shifted)
    exp_total = jnp.sum(weights, axis=1)
    spread = jnp.sum(weights * shifted, axis=1)
    columns = first_col + lax.iota(jnp.int32, logits.shape[1])
    target_logit = jnp.sum(jnp.where(columns[None, :] == block_ids[:, None], logits, 0.0), axis=1)
    return (peak, exp_total, spread, target_logit)


def combine(earlier, later):
    peak = jnp.maximum(earlier[0], later[0])
    left_lift = jnp.exp(earlier[0] - peak)
    right_lift = jnp.exp(later[0] - peak)
    exp_total = earlier[1] * left_lift + later[1] * right_lift
    spread = left_lift * (earlier[2] + (earlier[0] - peak) * earlier[1]) + right_lift * (
        later[2] + (later[0] - peak) * later[1]
    )
    return (peak, exp_total, spread, earlier[3] + later[3])


def per_device(hidden, norm_gain, head_weight, targets, pad_mask, lengths):
    width_count = lax.axis_size("width")
    own_count = targets.shape[0]
    values = hidden.astype(jnp.float32)
    energy = lax.psum(jnp.sum(values * values, axis=1), "width")
    inv_rms = lax.rsqrt(energy / (hidden.shape[1] * width_count) + epsilon)
    normed = (values * inv_rms[:, None] * norm_gain.astype(jnp.float32)[None, :]).astype(
        jnp.bfloat16
    )
    full_rows = lax.all_to_all(normed, "width", split_axis=0, concat_axis=1, tiled=True)
    gathered, gathered_ids = (
        lax.all_gather(full_rows, "vocab", axis=0, tiled=True),
        lax.all_gather(targets, "vocab", axis=0, tiled=True),
    )
    col_count = head_weight.shape[0]
    first_col = lax.axis_index("vocab") * col_count
    total_rows = gathered.shape[0]
    block_rows = math.gcd(total_rows, 512)
    contract = (((1,), (1,)), ((), ()))
    head_full = lax.all_gather(head_weight, "width", axis=1, tiled=True)

    def per_block(inputs):
        logits = lax.dot_general(inputs[0], head_full, contract, preferred_element_type=jnp.float32)
        return summarize(logits, inputs[1], first_col)

    blocked = lax.map(
        per_block,
        (gathered.reshape(-1, block_rows, gathered.shape[1]), gathered_ids.reshape(-1, block_rows)),
    )
    statistics = (
        blocked[0].reshape(-1),
        blocked[1].reshape(-1),
        blocked[2].reshape(-1),
        blocked[3].reshape(-1),
    )
    merged = merged_2(statistics, "vocab", combine)
    own_start = lax.axis_index("vocab") * own_count
    peak = lax.dynamic_slice_in_dim(merged[0], own_start, own_count, 0)
    exp_total = lax.dynamic_slice_in_dim(merged[1], own_start, own_count, 0)
    spread = lax.dynamic_slice_in_dim(merged[2], own_start, own_count, 0)
    target_logit = lax.dynamic_slice_in_dim(merged[3], own_start, own_count, 0)
    kept_mask = pad_mask.astype(jnp.float32)
    log_total = jnp.log(exp_total)
    entropy = kept_mask * (log_total - spread / exp_total)
    token_logprob = kept_mask * (target_logit - peak - log_total)
    device_index = lax.axis_index("vocab") * width_count + lax.axis_index("width")
    token_index = device_index * own_count + lax.iota(jnp.int32, own_count)
    seq_ends = jnp.cumsum(lengths)
    seq_starts = seq_ends - lengths
    member = (
        (token_index[:, None] >= seq_starts[None, :]) & (token_index[:, None] < seq_ends[None, :])
    ).astype(jnp.float32)
    partial_value = jnp.sum(member * token_logprob[:, None], axis=0)
    seq_score = lax.psum(partial_value, ("vocab", "width")) / lengths.astype(jnp.float32)
    return (entropy, token_logprob, seq_score)


def solution(mesh):
    placed = (
        P("vocab", "width"),
        P("width"),
        P("vocab", "width"),
        P(("vocab", "width")),
        P(("vocab", "width")),
        P(),
    )
    return jax.shard_map(
        per_device,
        mesh=mesh,
        in_specs=placed,
        out_specs=(P(("vocab", "width")), P(("vocab", "width")), P()),
        check_vma=False,
    )
```

profile of v0, /device:TPU:1, one launch (start us, length us, event | category | flops | bytes accessed | tf_op | source)
XLA Modules:
  0.0 491.1 jit_solution(4575408305845917003)
XLA Ops:
  7.2 0.0 all-gather.7.cloned.1.call-start
  7.2 0.9 fusion.5
  8.2 20.3 %psum.14 = f32[128]{0:T(128)S(1)} all-reduce(f32[128]{0:T(128)S(1)} %fusion.5), channel_id=1, replica_groups=mesh['vocab'=64,'width'=8] {'width'}, use_global_device_ids=true, to_apply=%region_1.0 | all-reduce | flops 128 | bytes 1024 | tf_op jit(solution)/shard_map/psum | solution.py:44
  28.4 0.7 convert_element_type.18
  29.1 0.9 fusion.7
  30.0 9.6 %all_to_all.19 = bf16[8,16,256]{2,1,0:T(8,128)(2,1)S(1)} all-to-all(bf16[8,16,256]{2,1,0:T(8,128)(2,1)S(1)} %bitcast.73), channel_id=1, replica_groups=mesh['vocab'=64,'width'=8] {'width'}, dimensions={0} | all-to-all | bytes 131072 | tf_op jit(solution)/shard_map/all_to_all | solution.py:49
  39.6 0.6 copy.21
  40.2 0.0 all-gather.7.cloned.1.call-update
  40.3 0.0 all-gather.9.cloned.1.call-start
  40.3 0.7 all-gather.9.cloned.1.call-update
  41.1 1.3 dynamic-slice
  43.0 0.9 dynamic-update-slice
  43.9 22.5 %all-reduce = s32[1024]{0:T(1024)S(1)} all-reduce(s32[1024]{0:T(1024)S(1)} %dynamic-update-slice), channel_id=1, replica_groups=mesh['vocab'=64,'width'=8] {'vocab'}, use_global_device_ids=true, to_apply=%add | all-reduce | flops 1024 | bytes 8192
  66.4 0.7 copy.16
  67.2 0.1 reduce-window.8
  67.3 0.1 reduce
  67.4 0.7 sub.31
  68.0 58.4 %all-gather.7.cloned.1.call-done = bf16[1024,2048]{1,0:T(8,128)(2,1)} async-done(((bf16[16,2048]{1,0:T(8,128)(2,1)}), bf16[1024,2048]{1,0:T(8,128)(2,1)}) %all-gather.7.cloned.1.call-update) | async-done | bytes 4194320 | tf_op jit(solution)/shard_map/all_gather | solution.py:51
  126.4 83.2 %all-gather.9.cloned.1.call-done = bf16[1600,2048]{1,0:T(8,128)(2,1)} async-done(((bf16[1600,256]{1,0:T(8,128)(2,1)}), bf16[1600,2048]{1,0:T(8,128)(2,1)}) %all-gather.9.cloned.1.call-update) | async-done | bytes 6553616 | tf_op jit(solution)/shard_map/all_gather | solution.py:59
  209.6 16.2 %while.32 = (s32[]{:T(128)}, f32[2,512]{1,0:T(2,128)S(1)}, f32[2,512]{1,0:T(2,128)S(1)}, f32[2,512]{1,0:T(2,128)S(1)}, f32[2,512]{1,0:T(2,128)S(1)}, /*index=5*/...) while((s32[]{:T(128)}, f32[2,512]{1,0:T(2,128)S(1)}, ...), condition=%wide.region_7.8_spmd, body=%wide.region_2.7_spmd.sunk | while | flops 3361996288 | bytes 15250565 | solution.py:65
  209.6 6.4 %fusion.14 = (f32[512]{0:T(512)S(1)}, f32[512,1600]{0,1:T(8,128)S(1)}) fusion(bf16[1600,2048]{1,0:T(8,128)(2,1)} %get-tuple-element.320, bf16[2,512,2048]{2,1,0:T(8,128)(2,1)} %get-tuple-element.319, s32[]{:T(128)} %get-tuple-element.303), kind=kOutput, calls=%fused_computation.31.clone.1 | convolution fusion | flops 3356261888 | bytes 11930112 | tf_op jit(solution)/shard_map/while/body/eval_jaxpr/dot_general | solution.py:62
  216.1 1.4 fusion.15
  217.7 6.4 %fusion.14 = (f32[512]{0:T(512)S(1)}, f32[512,1600]{0,1:T(8,128)S(1)}) fusion(bf16[1600,2048]{1,0:T(8,128)(2,1)} %get-tuple-element.320, bf16[2,512,2048]{2,1,0:T(8,128)(2,1)} %get-tuple-element.319, s32[]{:T(128)} %get-tuple-element.303), kind=kOutput, calls=%fused_computation.31.clone.1 | convolution fusion | flops 3356261888 | bytes 11930112 | tf_op jit(solution)/shard_map/while/body/eval_jaxpr/dot_general | solution.py:62
  224.2 1.4 fusion.15
  225.8 0.0 copy-start.2
  225.8 0.0 copy-start.1
  225.8 42.7 %all-gather = f32[64,1,1024]{2,1,0:T(1,128)S(1)} all-gather(f32[1,1,1024]{2,1,0:T(1,128)S(1)} %reshape.60), channel_id=1, replica_groups=mesh['vocab'=64,'width'=8] {'vocab'}, dimensions={0}, use_global_device_ids=true | all-gather | bytes 266240 | tf_op jit(solution)/shard_map/all_gather | solution.py:11
  268.6 37.2 %all-gather.1 = f32[64,1,1024]{2,1,0:T(1,128)S(1)} all-gather(f32[1,1,1024]{2,1,0:T(1,128)S(1)} %reshape.62), channel_id=1, replica_groups=mesh['vocab'=64,'width'=8] {'vocab'}, dimensions={0}, use_global_device_ids=true | all-gather | bytes 266240 | tf_op jit(solution)/shard_map/all_gather | solution.py:11
  305.8 36.9 %all-gather.2 = f32[64,1,1024]{2,1,0:T(1,128)S(1)} all-gather(f32[1,1,1024]{2,1,0:T(1,128)S(1)} %reshape.64), channel_id=1, replica_groups=mesh['vocab'=64,'width'=8] {'vocab'}, dimensions={0}, use_global_device_ids=true | all-gather | bytes 266240 | tf_op jit(solution)/shard_map/all_gather | solution.py:11
  342.7 37.1 %all-gather.3 = f32[64,1,1024]{2,1,0:T(1,128)S(1)} all-gather(f32[1,1,1024]{2,1,0:T(1,128)S(1)} %reshape.66), channel_id=1, replica_groups=mesh['vocab'=64,'width'=8] {'vocab'}, dimensions={0}, use_global_device_ids=true | all-gather | bytes 266240 | tf_op jit(solution)/shard_map/all_gather | solution.py:11
  380.2 7.6 %while.33 = (s32[]{:T(128)}, f32[1024]{0:T(1024)S(1)}, f32[1024]{0:T(1024)S(1)}, f32[1024]{0:T(1024)S(1)}, f32[1024]{0:T(1024)S(1)}, /*index=5*/f32[63,1024]{1,0...) while((s32[]{:T(128)}, f32[1024]{0:T(1024)S(1)}, ...), condition=%wide.region_9.10_spmd, body=%wide.region_8.9_spmd.sunk | while | flops 16386 | bytes 110701 | solution.py:14
  387.7 0.0 copy-done.2
  387.7 0.6 subtract_multiply_fusion
  388.3 0.0 copy-start
  388.3 0.1 select_reduce_fusion.1
  388.4 95.3 %psum.15 = f32[64]{0:T(128)S(1)} all-reduce(f32[64]{0:T(128)S(1)} %select_reduce_fusion.1), channel_id=1, replica_groups=mesh['vocab'=64,'width'=8] {'vocab','width'}, use_global_device_ids=true, to_apply=%region_12.13 | all-reduce | flops 64 | bytes 512 | tf_op jit(solution)/shard_map/psum | solution.py:93
  483.7 0.0 copy-done.1
  483.7 0.5 convert_divide_fusion
  484.2 0.0 copy-done
  (414 shorter events, 4.6 us)
Async XLA Ops:
  7.2 119.3 %all-gather.7.cloned.1.call-start = ((), (), s32[]{:S(2)}) async-start(), calls=%async_computation.1 | async-start | bytes 4259840 | tf_op jit(solution)/shard_map/all_gather | solution.py:51
  40.3 169.3 %all-gather.9.cloned.1.call-start = ((), (), s32[]{:S(2)}) async-start(), calls=%async_computation.2 | async-start | bytes 7372800 | tf_op jit(solution)/shard_map/all_gather | solution.py:59
  225.8 162.0 %copy-start.2 = (s32[16]{0:T(128)S(1)}, s32[16]{0:T(128)}, u32[]{:S(2)}) copy-start(s32[16]{0:T(128)} %param.14) | copy-start | bytes 196
  225.8 257.9 %copy-start.1 = (s32[64]{0:T(128)S(1)}, s32[64]{0:T(128)}, u32[]{:S(2)}) copy-start(s32[64]{0:T(128)} %param.15) | copy-start | bytes 772
  388.3 95.9 %copy-start = (f32[16]{0:T(128)}, f32[16]{0:T(128)S(1)}, u32[]{:S(2)}) copy-start(f32[16]{0:T(128)S(1)} %get-tuple-element.158) | copy-start | bytes 196
Sparse Core Ops, SparseCore 0:
  40.4 85.9 all-gather.6
  128.4 81.1 all-gather.8
where the time goes:
time: 491 us
  blocking collectives  302 us (62%)
  waiting for transfers between devices  142 us (29%)
  between operations  14.9 us (3%)
  matrix products  12.9 us (3%)
  other arithmetic  9.19 us (2%)
  local copies, waits for them, and re-layouts  6.36 us (1%)
    all_gather x4, blocking collectives, merged_2(): pieces = jax.tree.map(lambda part: lax.all_gather(part, axis), value)  154 us
    psum x1, blocking collectives, per_device(): lax.psum(partial_value, ('vocab', 'width')) / lengths.astype(jnp.float32)  95.3 us
    all_gather x1, waiting for transfers between devices, per_device(): head_full = lax.all_gather(head_weight, 'width', axis=1, tiled=True)  83.2 us
    all_gather x1, waiting for transfers between devices, per_device(): lax.all_gather(full_rows, 'vocab', axis=0, tiled=True)  58.4 us
    unnamed x1, blocking collectives  22.5 us
    psum x1, blocking collectives, per_device(): energy = lax.psum(jnp.sum(values * values, axis=1), 'width')  20.3 us
    dot_general x2, matrix products, per_block(): lax.dot_general(inputs[0], head_full, contract, preferred_element_type=jn...  12.9 us
  transfers between devices with their start and end apart: 2, of which 2 were waited for; matrix products, arithmetic and copies ran while one was open for 1% of the time, Pallas kernels for 0%

commit v1 on v0

--- a/solution.py
+++ b/solution.py
@@ -5,6 +5,11 @@
 from jax.sharding import PartitionSpec as P
 
 epsilon = 1e-06
+
+
+def axis_by_axis(value_2, first, second):
+    half = lax.psum(value_2, first)
+    return lax.psum(half, second)
 
 
 def merged_2(value, axis, join):
@@ -90,7 +95,7 @@
         (token_index[:, None] >= seq_starts[None, :]) & (token_index[:, None] < seq_ends[None, :])
     ).astype(jnp.float32)
     partial_value = jnp.sum(member * token_logprob[:, None], axis=0)
-    seq_score = lax.psum(partial_value, ("vocab", "width")) / lengths.astype(jnp.float32)
+    seq_score = axis_by_axis(partial_value, "vocab", "width") / lengths.astype(jnp.float32)
     return (entropy, token_logprob, seq_score)
 
 

time: 491 us -> 536 us (1.092)
  blocking collectives: 302 us -> 342 us
    psum x1 -> x2, blocking collectives: 95.3 us -> 136 us  [the longest x1 123 us: axis_by_axis(): half = lax.psum(value_2, first)]
where the time goes in v1:
time: 536 us; the launch traced here: 532 us
  blocking collectives  342 us (64%)
  waiting for transfers between devices  142 us (26%)
  between operations  14.9 us (3%)
  matrix products  12.9 us (2%)
  other arithmetic  9.19 us (2%)
  local copies, waits for them, and re-layouts  6.36 us (1%)
    all_gather x4, blocking collectives, merged_2(): pieces = jax.tree.map(lambda part: lax.all_gather(part, axis), value)  154 us
    psum x1, blocking collectives, axis_by_axis(): half = lax.psum(value_2, first)  123 us
    all_gather x1, waiting for transfers between devices, per_device(): head_full = lax.all_gather(head_weight, 'width', axis=1, tiled=True)  83.2 us
    all_gather x1, waiting for transfers between devices, per_device(): lax.all_gather(full_rows, 'vocab', axis=0, tiled=True)  58.4 us
    unnamed x1, blocking collectives  22.5 us
    psum x1, blocking collectives, per_device(): energy = lax.psum(jnp.sum(values * values, axis=1), 'width')  20.3 us
    dot_general x2, matrix products, per_block(): lax.dot_general(inputs[0], head_full, contract, preferred_element_type=jn...  12.9 us
    psum x1, blocking collectives, axis_by_axis(): return lax.psum(half, second)  12.3 us
  transfers between devices with their start and end apart: 2, of which 2 were waited for; matrix products, arithmetic and copies ran while one was open for 1% of the time, Pallas kernels for 0%

profile of v1, /device:TPU:1, one launch (start us, length us, event | category | flops | bytes accessed | tf_op | source)
XLA Modules:
  0.0 531.5 jit_solution(14616874720523221621)
XLA Ops:
  7.2 0.0 all-gather.7.cloned.1.call-start
  7.2 0.9 fusion.5
  8.2 20.3 %psum.21 = f32[128]{0:T(128)S(1)} all-reduce(f32[128]{0:T(128)S(1)} %fusion.5), channel_id=1, replica_groups=mesh['vocab'=64,'width'=8] {'width'}, use_global_device_ids=true, to_apply=%region_1.0 | all-reduce | flops 128 | bytes 1024 | tf_op jit(solution)/shard_map/psum | solution.py:49
  28.4 0.7 convert_element_type.18
  29.1 0.9 fusion.7
  30.0 9.6 %all_to_all.19 = bf16[8,16,256]{2,1,0:T(8,128)(2,1)S(1)} all-to-all(bf16[8,16,256]{2,1,0:T(8,128)(2,1)S(1)} %bitcast.73), channel_id=1, replica_groups=mesh['vocab'=64,'width'=8] {'width'}, dimensions={0} | all-to-all | bytes 131072 | tf_op jit(solution)/shard_map/all_to_all | solution.py:54
  39.6 0.6 copy.21
  40.2 0.0 all-gather.7.cloned.1.call-update
  40.3 0.0 all-gather.9.cloned.1.call-start
  40.3 0.7 all-gather.9.cloned.1.call-update
  41.1 1.3 dynamic-slice
  43.0 0.9 dynamic-update-slice
  43.9 22.5 %all-reduce = s32[1024]{0:T(1024)S(1)} all-reduce(s32[1024]{0:T(1024)S(1)} %dynamic-update-slice), channel_id=1, replica_groups=mesh['vocab'=64,'width'=8] {'vocab'}, use_global_device_ids=true, to_apply=%add | all-reduce | flops 1024 | bytes 8192
  66.4 0.7 copy.16
  67.2 0.1 reduce-window.8
  67.3 0.1 reduce
  67.4 0.7 sub.31
  68.0 58.4 %all-gather.7.cloned.1.call-done = bf16[1024,2048]{1,0:T(8,128)(2,1)} async-done(((bf16[16,2048]{1,0:T(8,128)(2,1)}), bf16[1024,2048]{1,0:T(8,128)(2,1)}) %all-gather.7.cloned.1.call-update) | async-done | bytes 4194320 | tf_op jit(solution)/shard_map/all_gather | solution.py:56
  126.4 83.2 %all-gather.9.cloned.1.call-done = bf16[1600,2048]{1,0:T(8,128)(2,1)} async-done(((bf16[1600,256]{1,0:T(8,128)(2,1)}), bf16[1600,2048]{1,0:T(8,128)(2,1)}) %all-gather.9.cloned.1.call-update) | async-done | bytes 6553616 | tf_op jit(solution)/shard_map/all_gather | solution.py:64
  209.6 16.2 %while.32 = (s32[]{:T(128)}, f32[2,512]{1,0:T(2,128)S(1)}, f32[2,512]{1,0:T(2,128)S(1)}, f32[2,512]{1,0:T(2,128)S(1)}, f32[2,512]{1,0:T(2,128)S(1)}, /*index=5*/...) while((s32[]{:T(128)}, f32[2,512]{1,0:T(2,128)S(1)}, ...), condition=%wide.region_7.8_spmd, body=%wide.region_2.7_spmd.sunk | while | flops 3361996288 | bytes 15250565 | solution.py:70
  209.6 6.4 %fusion.14 = (f32[512]{0:T(512)S(1)}, f32[512,1600]{0,1:T(8,128)S(1)}) fusion(bf16[1600,2048]{1,0:T(8,128)(2,1)} %get-tuple-element.320, bf16[2,512,2048]{2,1,0:T(8,128)(2,1)} %get-tuple-element.319, s32[]{:T(128)} %get-tuple-element.303), kind=kOutput, calls=%fused_computation.31.clone.1 | convolution fusion | flops 3356261888 | bytes 11930112 | tf_op jit(solution)/shard_map/while/body/eval_jaxpr/dot_general | solution.py:67
  216.1 1.4 fusion.15
  217.7 6.4 %fusion.14 = (f32[512]{0:T(512)S(1)}, f32[512,1600]{0,1:T(8,128)S(1)}) fusion(bf16[1600,2048]{1,0:T(8,128)(2,1)} %get-tuple-element.320, bf16[2,512,2048]{2,1,0:T(8,128)(2,1)} %get-tuple-element.319, s32[]{:T(128)} %get-tuple-element.303), kind=kOutput, calls=%fused_computation.31.clone.1 | convolution fusion | flops 3356261888 | bytes 11930112 | tf_op jit(solution)/shard_map/while/body/eval_jaxpr/dot_general | solution.py:67
  224.2 1.4 fusion.15
  225.8 0.0 copy-start.2
  225.8 0.0 copy-start.1
  225.8 42.7 %all-gather = f32[64,1,1024]{2,1,0:T(1,128)S(1)} all-gather(f32[1,1,1024]{2,1,0:T(1,128)S(1)} %reshape.60), channel_id=1, replica_groups=mesh['vocab'=64,'width'=8] {'vocab'}, dimensions={0}, use_global_device_ids=true | all-gather | bytes 266240 | tf_op jit(solution)/shard_map/all_gather | solution.py:16
  268.6 37.2 %all-gather.1 = f32[64,1,1024]{2,1,0:T(1,128)S(1)} all-gather(f32[1,1,1024]{2,1,0:T(1,128)S(1)} %reshape.62), channel_id=1, replica_groups=mesh['vocab'=64,'width'=8] {'vocab'}, dimensions={0}, use_global_device_ids=true | all-gather | bytes 266240 | tf_op jit(solution)/shard_map/all_gather | solution.py:16
  305.8 36.9 %all-gather.2 = f32[64,1,1024]{2,1,0:T(1,128)S(1)} all-gather(f32[1,1,1024]{2,1,0:T(1,128)S(1)} %reshape.64), channel_id=1, replica_groups=mesh['vocab'=64,'width'=8] {'vocab'}, dimensions={0}, use_global_device_ids=true | all-gather | bytes 266240 | tf_op jit(solution)/shard_map/all_gather | solution.py:16
  342.7 37.1 %all-gather.3 = f32[64,1,1024]{2,1,0:T(1,128)S(1)} all-gather(f32[1,1,1024]{2,1,0:T(1,128)S(1)} %reshape.66), channel_id=1, replica_groups=mesh['vocab'=64,'width'=8] {'vocab'}, dimensions={0}, use_global_device_ids=true | all-gather | bytes 266240 | tf_op jit(solution)/shard_map/all_gather | solution.py:16
  380.2 7.6 %while.33 = (s32[]{:T(128)}, f32[1024]{0:T(1024)S(1)}, f32[1024]{0:T(1024)S(1)}, f32[1024]{0:T(1024)S(1)}, f32[1024]{0:T(1024)S(1)}, /*index=5*/f32[63,1024]{1,0...) while((s32[]{:T(128)}, f32[1024]{0:T(1024)S(1)}, ...), condition=%wide.region_9.10_spmd, body=%wide.region_8.9_spmd.sunk | while | flops 16386 | bytes 110701 | solution.py:19
  387.7 0.0 copy-done.2
  387.7 0.6 subtract_multiply_fusion
  388.3 0.0 copy-start
  388.3 0.1 select_reduce_fusion.1
  388.4 123.4 %psum.22 = f32[64]{0:T(128)S(1)} all-reduce(f32[64]{0:T(128)S(1)} %select_reduce_fusion.1), channel_id=1, replica_groups=mesh['vocab'=64,'width'=8] {'vocab'}, use_global_device_ids=true, to_apply=%region_12.13 | all-reduce | flops 64 | bytes 512 | tf_op jit(solution)/shard_map/psum | solution.py:11
  511.8 12.3 %psum.23 = f32[64]{0:T(128)S(1)} all-reduce(f32[64]{0:T(128)S(1)} %psum.22), channel_id=1, replica_groups=mesh['vocab'=64,'width'=8] {'width'}, use_global_device_ids=true, to_apply=%region_13.14 | all-reduce | flops 64 | bytes 512 | tf_op jit(solution)/shard_map/psum | solution.py:12
  524.1 0.0 copy-done.1
  524.1 0.5 convert_divide_fusion
  524.7 0.0 copy-done
  (414 shorter events, 4.6 us)
Async XLA Ops:
  7.2 119.3 %all-gather.7.cloned.1.call-start = ((), (), s32[]{:S(2)}) async-start(), calls=%async_computation.1 | async-start | bytes 4259840 | tf_op jit(solution)/shard_map/all_gather | solution.py:56
  40.3 169.3 %all-gather.9.cloned.1.call-start = ((), (), s32[]{:S(2)}) async-start(), calls=%async_computation.2 | async-start | bytes 7372800 | tf_op jit(solution)/shard_map/all_gather | solution.py:64
  225.8 162.0 %copy-start.2 = (s32[16]{0:T(128)S(1)}, s32[16]{0:T(128)}, u32[]{:S(2)}) copy-start(s32[16]{0:T(128)} %param.14) | copy-start | bytes 196
  225.8 298.4 %copy-start.1 = (s32[64]{0:T(128)S(1)}, s32[64]{0:T(128)}, u32[]{:S(2)}) copy-start(s32[64]{0:T(128)} %param.15) | copy-start | bytes 772
  388.3 136.3 %copy-start = (f32[16]{0:T(128)}, f32[16]{0:T(128)S(1)}, u32[]{:S(2)}) copy-start(f32[16]{0:T(128)S(1)} %get-tuple-element.158) | copy-start | bytes 196
Sparse Core Ops, SparseCore 0:
  40.4 85.9 all-gather.6
  128.4 81.1 all-gather.8
